TPU v7x, 256 devices: a whole 4x4x8 slice. The times are simulated.
256 devices in a mesh: section: 4 (over x_lo, core), row: 8 (over z), col: 8 (over x_hi, y).
Axes of the slice: x: 4 (x_hi: 2, x_lo: 2; x = x_hi * 2 + x_lo), y: 4, z: 8, core: 2. Of those that a mesh axis runs over, the one named last changes fastest.
Arguments:
- images: bfloat16 [4, 8, 80, 80, 512], P('section', None, 'row', 'col'), may hold values from -6 to 6
- block_in: bfloat16 [512, 256], replicated, may hold values from -0.25 to 0.25
- block_grouped_one: bfloat16 [1152, 256], replicated, may hold values from -0.1875 to 0.1875
- block_grouped_two: bfloat16 [1152, 256], replicated, may hold values from -0.1875 to 0.1875
- block_out: bfloat16 [256, 512], replicated, may hold values from -0.375 to 0.375
- trans_in: bfloat16 [512, 768], replicated, may hold values from -0.25 to 0.25
- trans_grouped_one: bfloat16 [1152, 768], replicated, may hold values from -0.1875 to 0.1875
- trans_grouped_two: bfloat16 [1152, 768], replicated, may hold values from -0.1875 to 0.1875
- trans_out: bfloat16 [768, 1536], replicated, may hold values from -0.21875 to 0.21875
- trans_short: bfloat16 [512, 1536], replicated, may hold values from -0.25 to 0.25
Outputs:
- features: bfloat16 [4, 8, 40, 40, 1536], P('section', 'row', 'col')
All inputs are finite; a program needn't handle non-finite values.
Results may differ from a plain program's by a relative error of at most 0.012.
Values may be sent and summed in bfloat16 or wider, within the bound.
A program may use at most 64 MiB of HBM per device.

v0:
```python
import functools

import jax
import jax.numpy as jnp
from jax import lax
from jax.experimental import pallas as pl
from jax.experimental.pallas import tpu as pltpu
from jax.sharding import PartitionSpec as P

GELU_GAIN = 1.7015
RESIDUAL_SCALE = 0.2
BETA_BLOCK = 0.9805
BETA_TRANSITION = 0.9623
GROUP = 128
MESH = pl.DeviceIdType.MESH

TOP = 4
BOTTOM = 5


def activate(values):
    return GELU_GAIN * jax.nn.gelu(values, approximate=True)


def gather_kernel(nrow, ncol, img_ref, out_ref, send_sem, recv_sem):
    s = lax.axis_index("section")
    r = lax.axis_index("row")
    c = lax.axis_index("col")
    n_img, th, tw = img_ref.shape[0], img_ref.shape[1], img_ref.shape[2]
    barrier = pltpu.get_barrier_semaphore()

    dests = []
    for i in range(n_img):
        for k, delta in enumerate((-1, 0, 1)):
            valid = jnp.logical_and(r + delta >= 0, r + delta < ncol)
            cd = lax.rem(r + delta + ncol, ncol)
            is_self = jnp.logical_and(r == i, cd == c)
            dests.append((i, k, delta, cd, valid, is_self))
    sources = []
    for d in range(3):
        for cs in range(ncol):
            valid = jnp.logical_and(c + d - 1 >= 0, c + d - 1 < nrow)
            rs = lax.rem(c + d - 1 + nrow, nrow)
            is_self = jnp.logical_and(rs == r, cs == c)
            sources.append((d, cs, rs, valid, is_self))

    def remote(valid, is_self):
        return jnp.logical_and(valid, jnp.logical_not(is_self))

    for i, k, delta, cd, valid, is_self in dests:
        @pl.when(remote(valid, is_self))
        def _():
            pl.semaphore_signal(barrier, 1, device_id=(s, i, cd), device_id_type=MESH)
    for d, cs, rs, valid, is_self in sources:
        @pl.when(remote(valid, is_self))
        def _():
            pl.semaphore_signal(barrier, 1, device_id=(s, rs, cs), device_id_type=MESH)
    peers = [remote(valid, is_self) for _, _, _, _, valid, is_self in dests]
    peers += [remote(valid, is_self) for _, _, _, valid, is_self in sources]
    pl.semaphore_wait(barrier, sum(p.astype(jnp.int32) for p in peers))

    spans = {0: (0, th, TOP), 1: (th - TOP, TOP, 0), -1: (0, BOTTOM, TOP + th)}
    remote_copies = []
    for i, k, delta, cd, valid, is_self in dests:
        r0, n, d0 = spans[delta]
        src = img_ref.at[i, pl.ds(r0, n)]
        dst = out_ref.at[pl.ds(d0, n), c]
        slot = 1 - delta
        rdesc = pltpu.make_async_remote_copy(
            src_ref=src,
            dst_ref=dst,
            send_sem=send_sem.at[i, k],
            recv_sem=recv_sem.at[slot, c],
            device_id=(s, i, cd),
            device_id_type=MESH,
        )
        ldesc = pltpu.make_async_copy(src, dst, recv_sem.at[slot, c])
        is_remote = remote(valid, is_self)

        @pl.when(is_remote)
        def _():
            rdesc.start()

        @pl.when(jnp.logical_and(valid, is_self))
        def _():
            ldesc.start()

        remote_copies.append((rdesc, is_remote))

    lands = {0: (TOP, 0), 1: (th, TOP), 2: (BOTTOM, TOP + th)}
    for d, cs, rs, valid, is_self in sources:
        n, d0 = lands[d]
        dst = out_ref.at[pl.ds(d0, n), cs]
        desc = pltpu.make_async_copy(dst, dst, recv_sem.at[d, cs])

        @pl.when(valid)
        def _():
            desc.wait()

    for rdesc, is_remote in remote_copies:
        @pl.when(is_remote)
        def _():
            rdesc.wait_send()


def gather_strips(tiles, nrow, ncol):
    n_img, th, tw, ch = tiles.shape
    return pl.pallas_call(
        functools.partial(gather_kernel, nrow, ncol),
        out_shape=jax.ShapeDtypeStruct((TOP + th + BOTTOM, ncol, tw, ch), tiles.dtype),
        in_specs=[pl.BlockSpec(memory_space=pl.ANY)],
        out_specs=pl.BlockSpec(memory_space=pl.ANY),
        scratch_shapes=[
            pltpu.SemaphoreType.DMA((n_img, 3)),
            pltpu.SemaphoreType.DMA((3, ncol)),
        ],
        compiler_params=pltpu.CompilerParams(collective_id=0, has_side_effects=True),
    )(tiles)


def tap_weights(weight):
    channels = weight.shape[1]
    return weight.reshape(3, 3, GROUP, channels).transpose(1, 0, 2, 3).reshape(3, 3 * GROUP, channels)


def inside_rows(count, width, first, height):
    rows = first + lax.broadcasted_iota(jnp.int32, (count * width, 1), 0) // width
    return jnp.logical_and(rows >= 0, rows < height)


def column_of(count, width):
    return lax.broadcasted_iota(jnp.int32, (count * width, 1), 0) % width


def conv_taps(rows_of, out_rows, width, w_ref, group):
    sl = slice(group * GROUP, (group + 1) * GROUP)
    slab = jnp.concatenate([rows_of(a)[:, :, sl] for a in range(3)], axis=-1)
    slab = slab.reshape(out_rows * width, 3 * GROUP).astype(jnp.bfloat16)
    return [jnp.dot(slab, w_ref[b, :, sl], preferred_element_type=jnp.float32) for b in range(3)]


def conv_same(x, w_ref):
    in_rows, width, channels = x.shape
    out_rows = in_rows - 2
    n = out_rows * width
    col = column_of(out_rows, width)
    outs = []
    for g in range(channels // GROUP):
        y = conv_taps(lambda a: x[a : a + out_rows], out_rows, width, w_ref, g)
        left = jnp.where(col == 0, 0.0, pltpu.roll(y[0], 1, 0))
        right = jnp.where(col == width - 1, 0.0, pltpu.roll(y[2], n - 1, 0))
        outs.append(y[1] + left + right)
    return jnp.concatenate(outs, axis=-1)


def block_kernel(base_ref, x_ref, win_ref, w1_ref, w2_ref, wout_ref, o_ref):
    rows, width, ch = x_ref.shape
    height = base_ref[1]
    base = base_ref[0]
    x = x_ref[...].astype(jnp.float32).reshape(rows * width, ch)
    pre = (activate(x) * BETA_BLOCK).astype(jnp.bfloat16)
    first = activate(jnp.dot(pre, win_ref[...], preferred_element_type=jnp.float32))
    first = jnp.where(inside_rows(rows, width, base, height), first, 0.0)
    first = first.astype(jnp.bfloat16).astype(jnp.float32).reshape(rows, width, -1)
    second = activate(conv_same(first, w1_ref))
    second = jnp.where(inside_rows(rows - 2, width, base + 1, height), second, 0.0)
    second = second.astype(jnp.bfloat16).astype(jnp.float32).reshape(rows - 2, width, -1)
    third = activate(conv_same(second, w2_ref)).astype(jnp.bfloat16)
    skip = x_ref[2 : rows - 2].astype(jnp.float32).reshape((rows - 4) * width, ch)
    out = skip + RESIDUAL_SCALE * jnp.dot(third, wout_ref[...], preferred_element_type=jnp.float32)
    o_ref[...] = out.astype(o_ref.dtype).reshape(rows - 4, width, ch)


def trans_kernel(base_ref, x_ref, win_ref, w1_ref, w2_ref, wout_ref, wshort_ref, o_ref, pool_scr, sub_scr):
    rows, width, ch = x_ref.shape
    core_rows = rows - 5
    half = width // 2
    height = base_ref[1]
    base = base_ref[0] + 2
    x = x_ref[...].astype(jnp.float32).reshape(rows * width, ch)
    pre = (activate(x) * BETA_TRANSITION).astype(jnp.bfloat16)

    core = pre.astype(jnp.float32).reshape(rows, width, ch)[2 : 2 + core_rows]
    core = core.reshape(core_rows // 2, 2, width, ch)
    summed = (core[:, 0] + core[:, 1]).reshape(core_rows // 2 * width, ch)
    n_pool = core_rows // 2 * half
    parts = []
    for k in range(ch // GROUP):
        pool_scr[k] = summed[:, k * GROUP : (k + 1) * GROUP]
        part = pool_scr.at[k]
        parts.append(part[pl.ds(0, n_pool, stride=2), :] + part[pl.ds(1, n_pool, stride=2), :])
    pooled = (jnp.concatenate(parts, axis=-1) * 0.25).astype(jnp.bfloat16)

    first = activate(jnp.dot(pre, win_ref[...], preferred_element_type=jnp.float32))
    first = jnp.where(inside_rows(rows, width, base, height), first, 0.0)
    first = first.astype(jnp.bfloat16).astype(jnp.float32).reshape(rows, width, -1)
    mid = first.shape[-1]
    first = jnp.concatenate([first, jnp.zeros((1, width, mid), jnp.float32)], axis=0)
    pairs = first.reshape((rows + 1) // 2, 2, width, mid)
    out_rows = (rows - 1) // 2
    picks = (pairs[:out_rows, 0], pairs[:out_rows, 1], pairs[1 : out_rows + 1, 0])
    n = out_rows * width
    col = column_of(out_rows, width)
    for g in range(mid // GROUP):
        y = conv_taps(lambda a: picks[a], out_rows, width, w1_ref, g)
        z = y[0] + pltpu.roll(y[1], n - 1, 0) + jnp.where(col >= width - 2, 0.0, pltpu.roll(y[2], n - 2, 0))
        sub_scr[g, pl.ds(0, n), :] = z
    picked = [sub_scr.at[g][pl.ds(0, out_rows * half, stride=2), :] for g in range(mid // GROUP)]
    second = activate(jnp.concatenate(picked, axis=-1))
    second = jnp.where(inside_rows(out_rows, half, base_ref[0] // 2 + 1, height // 2), second, 0.0)
    second = second.astype(jnp.bfloat16).astype(jnp.float32).reshape(out_rows, half, mid)
    third = activate(conv_same(second, w2_ref)).astype(jnp.bfloat16)
    out = jnp.dot(pooled, wshort_ref[...], preferred_element_type=jnp.float32)
    out = out + RESIDUAL_SCALE * jnp.dot(third, wout_ref[...], preferred_element_type=jnp.float32)
    o_ref[...] = out.astype(o_ref.dtype)


def vmem_call(kernel, out_shape, n_in, scratch=()):
    return pl.pallas_call(
        kernel,
        out_shape=out_shape,
        in_specs=[pl.BlockSpec(memory_space=pltpu.SMEM)] + [pl.BlockSpec(memory_space=pltpu.VMEM)] * n_in,
        out_specs=pl.BlockSpec(memory_space=pltpu.VMEM),
        scratch_shapes=list(scratch),
    )


def compute(strip, base_info, block_in, block_grouped_one, block_grouped_two, block_out,
            trans_in, trans_grouped_one, trans_grouped_two, trans_out, trans_short):
    rows, width, ch = strip.shape
    block_result = vmem_call(block_kernel, jax.ShapeDtypeStruct((rows - 4, width, ch), jnp.bfloat16), 5)(
        base_info, strip, block_in, tap_weights(block_grouped_one), tap_weights(block_grouped_two), block_out
    )
    t_rows = rows - 4
    core_rows = t_rows - 5
    out_rows = (t_rows - 1) // 2
    mid = trans_in.shape[1]
    wide = trans_out.shape[1]
    scratch = (
        pltpu.VMEM((ch // GROUP, core_rows // 2 * width, GROUP), jnp.float32),
        pltpu.VMEM((mid // GROUP, out_rows * width + 8, GROUP), jnp.float32),
    )
    out_shape = jax.ShapeDtypeStruct(((core_rows // 2) * (width // 2), wide), jnp.bfloat16)
    features = vmem_call(trans_kernel, out_shape, 6, scratch)(
        base_info, block_result, trans_in, tap_weights(trans_grouped_one), tap_weights(trans_grouped_two),
        trans_out, trans_short
    )
    return features.reshape(core_rows // 2, width // 2, wide)


def local(
    images,
    block_in,
    block_grouped_one,
    block_grouped_two,
    block_out,
    trans_in,
    trans_grouped_one,
    trans_grouped_two,
    trans_out,
    trans_short,
):
    nrow = lax.axis_size("row")
    ncol = lax.axis_size("col")
    _, n_img, th, tw, ch = images.shape
    c = lax.axis_index("col")
    base_info = jnp.stack([c * th - TOP, th * nrow]).astype(jnp.int32)
    strip = gather_strips(images.reshape(n_img, th, tw, ch), nrow, ncol)
    strip = strip.reshape(TOP + th + BOTTOM, ncol * tw, ch)
    features = compute(strip, base_info, block_in, block_grouped_one, block_grouped_two, block_out,
                       trans_in, trans_grouped_one, trans_grouped_two, trans_out, trans_short)
    return features[None, None]


def solution(mesh):
    in_specs = (P("section", None, "row", "col", None), P(), P(), P(), P(), P(), P(), P(), P(), P())
    out_specs = P("section", "row", "col", None, None)
    return jax.shard_map(local, mesh=mesh, in_specs=in_specs, out_specs=out_specs, check_vma=False)
```

profile of v0, /device:TPU:92, one launch (start us, length us, event | category | flops | bytes accessed | tf_op | source)
XLA Modules:
  0.0 117.1 jit_solution(5114296101656415793)
XLA Ops:
  0.0 0.6 pad_add_fusion.base_ref
  0.6 2.6 %copy.24 = bf16[1,8,10,10,512]{4,3,2,1,0:T(8,128)(2,1)} copy(bf16[1,8,10,10,512]{4,1,3,2,0:T(8,128)(2,1)} %param.10) | data formatting | bytes 1638400 | tf_op args[0]
  3.2 82.6 %shard_map.100 = bf16[19,8,10,512]{3,2,1,0:T(8,128)(2,1)} custom-call(bf16[8,10,10,512]{3,2,1,0:T(8,128)(2,1)} %bitcast.25), custom_call_target="tpu_custom_call" | custom-call | tf_op jit(solution)/shard_map/pallas_call | solution.py:108
  85.8 2.7 %copy.17 = bf16[19,8,10,512]{3,0,2,1:T(8,128)(2,1)S(1)} copy(bf16[19,8,10,512]{3,2,1,0:T(8,128)(2,1)} %shard_map.100) | data formatting | bytes 3112960 | tf_op jit(solution)/shard_map/pallas_call | solution.py:108
  88.4 0.0 copy-start.2
  88.4 0.0 copy-start.3
  88.5 1.7 %copy.20.x_ref = bf16[19,80,512]{2,1,0:T(8,128)(2,1)} copy(bf16[19,80,512]{2,0,1:T(8,128)(2,1)S(1)} %bitcast.22) | data formatting | bytes 3112960 | tf_op jit(solution)/shard_map/reshape | solution.py:269
  90.1 0.0 copy-done.2
  90.2 0.9 copy.18
  91.0 0.0 copy-done.3
  91.0 0.9 copy.19
  91.9 0.0 copy-start
  91.9 10.0 %shard_map.101.x_ref = bf16[15,80,512]{2,1,0:T(8,128)(2,1)} custom-call(s32[2]{0:T(128)} %pad_add_fusion.base_ref, bf16[19,80,512]{2,1,0:T(8,128)(2,1)} %copy.20.x_ref, bf16[512,256]{1,0:T(8,128)(2,1)} %win_ref.2, bf16[3,384,256]{2,1,0:T(8,128)(2,1)} %bitcast.26, bf16[3,384,256]{2,1,0:T(8,128)(2,1)} %bitcast.27, bf16[256,512]{1,0:T(8,128)(2,1)} %wout_ref.2), custom_call_target="tpu_custom_call" | custom-call | tf_op jit(solution)/shard_map/pallas_call | solution.py:231
  101.9 0.0 copy-done
  101.9 0.0 copy-start.1
  101.9 1.4 %copy.21 = bf16[3,3,128,768]{3,2,0,1:T(8,128)(2,1)} copy(bf16[3,3,128,768]{3,2,1,0:T(8,128)(2,1)S(1)} %bitcast.28) | data formatting | bytes 3538944 | tf_op jit(solution)/shard_map/reshape | solution.py:123
  103.2 0.7 copy-done.1
  104.0 1.3 %copy.22 = bf16[3,3,128,768]{3,2,0,1:T(8,128)(2,1)} copy(bf16[3,3,128,768]{3,2,1,0:T(8,128)(2,1)S(1)} %bitcast.29) | data formatting | bytes 3538944 | tf_op jit(solution)/shard_map/reshape | solution.py:123
  105.3 11.8 %shard_map.102 = bf16[200,1536]{1,0:T(8,128)(2,1)} custom-call(s32[2]{0:T(128)} %pad_add_fusion.base_ref, bf16[15,80,512]{2,1,0:T(8,128)(2,1)} %shard_map.101.x_ref, bf16[512,768]{1,0:T(8,128)(2,1)} %win_ref.3, bf16[3,384,768]{2,1,0:T(8,128)(2,1)} %bitcast.23, bf16[3,384,768]{2,1,0:T(8,128)(2,1)} %bitcast.24, bf16[768,1536]{1,0:T(8,128)(2,1)} %wout_ref.3, ...), custom_call_target="tpu_custom_call" | custom-call | tf_op jit(solution)/shard_map/pallas_call | solution.py:244
Async XLA Ops:
  88.4 1.7 %copy-start.2 = (bf16[1152,256]{1,0:T(8,128)(2,1)S(1)}, bf16[1152,256]{1,0:T(8,128)(2,1)}, u32[]{:S(2)}) copy-start(bf16[1152,256]{1,0:T(8,128)(2,1)} %param.12) | copy-start | bytes 1769476
  88.4 2.6 %copy-start.3 = (bf16[1152,256]{1,0:T(8,128)(2,1)S(1)}, bf16[1152,256]{1,0:T(8,128)(2,1)}, u32[]{:S(2)}) copy-start(bf16[1152,256]{1,0:T(8,128)(2,1)} %param.13) | copy-start | bytes 1769476
  91.9 10.0 %copy-start = (bf16[1152,768]{1,0:T(8,128)(2,1)S(1)}, bf16[1152,768]{1,0:T(8,128)(2,1)}, u32[]{:S(2)}) copy-start(bf16[1152,768]{1,0:T(8,128)(2,1)} %param.16) | copy-start | bytes 5308420
  101.9 2.1 %copy-start.1 = (bf16[1152,768]{1,0:T(8,128)(2,1)S(1)}, bf16[1152,768]{1,0:T(8,128)(2,1)}, u32[]{:S(2)}) copy-start(bf16[1152,768]{1,0:T(8,128)(2,1)} %param.17) | copy-start | bytes 5308420
where the time goes:
time: 117 us
  Pallas kernels  104 us (89%)
  local copies, waits for them, and re-layouts  12.1 us (10%)
    pallas_call x1, Pallas kernels, gather_strips(): pl.pallas_call(functools.partial(gather_kernel, nrow, ncol), out_shape=ja...  82.6 us
    pallas_call x1, Pallas kernels, compute(): vmem_call(trans_kernel, out_shape, 6, scratch)  11.8 us
    pallas_call x1, Pallas kernels, compute(): vmem_call(block_kernel, jax.ShapeDtypeStruct((rows - 4, width, ch), jnp.b...  9.98 us
    reshape x4, local copies, waits for them, and re-layouts, tap_weights(): weight.reshape(3, 3, GROUP, channels).transpose(1, 0, 2, 3)  4.44 us
    unnamed x9, local copies, waits for them, and re-layouts  3.31 us
    pallas_call x1, local copies, waits for them, and re-layouts, gather_strips(): pl.pallas_call(functools.partial(gather_kernel, nrow, ncol), out_shape=ja...  2.66 us

commit v1 on v0

--- a/solution.py
+++ b/solution.py
@@ -22,7 +22,7 @@
     return GELU_GAIN * jax.nn.gelu(values, approximate=True)
 
 
-def gather_kernel(nrow, ncol, img_ref, out_ref, send_sem, recv_sem):
+def gather_kernel(nrow, ncol, img_ref, out_ref, send_sem, recv_sem, fwd_send, fwd_recv):
     s = lax.axis_index("section")
     r = lax.axis_index("row")
     c = lax.axis_index("col")
@@ -31,76 +31,107 @@
 
     dests = []
     for i in range(n_img):
-        for k, delta in enumerate((-1, 0, 1)):
-            valid = jnp.logical_and(r + delta >= 0, r + delta < ncol)
-            cd = lax.rem(r + delta + ncol, ncol)
-            is_self = jnp.logical_and(r == i, cd == c)
-            dests.append((i, k, delta, cd, valid, is_self))
+        is_self = jnp.logical_and(r == i, r == c)
+        dests.append((i, jnp.logical_not(is_self), is_self))
     sources = []
-    for d in range(3):
-        for cs in range(ncol):
-            valid = jnp.logical_and(c + d - 1 >= 0, c + d - 1 < nrow)
-            rs = lax.rem(c + d - 1 + nrow, nrow)
-            is_self = jnp.logical_and(rs == r, cs == c)
-            sources.append((d, cs, rs, valid, is_self))
-
-    def remote(valid, is_self):
-        return jnp.logical_and(valid, jnp.logical_not(is_self))
-
-    for i, k, delta, cd, valid, is_self in dests:
-        @pl.when(remote(valid, is_self))
-        def _():
-            pl.semaphore_signal(barrier, 1, device_id=(s, i, cd), device_id_type=MESH)
-    for d, cs, rs, valid, is_self in sources:
-        @pl.when(remote(valid, is_self))
-        def _():
-            pl.semaphore_signal(barrier, 1, device_id=(s, rs, cs), device_id_type=MESH)
-    peers = [remote(valid, is_self) for _, _, _, _, valid, is_self in dests]
-    peers += [remote(valid, is_self) for _, _, _, valid, is_self in sources]
+    for cs in range(ncol):
+        is_self = jnp.logical_and(c == r, cs == c)
+        sources.append((cs, jnp.logical_not(is_self)))
+    up = c - 1
+    down = c + 1
+    has_up = up >= 0
+    has_down = down < ncol
+    up_id = (s, r, lax.rem(up + ncol, ncol))
+    down_id = (s, r, lax.rem(down, ncol))
+
+    for i, is_remote, _ in dests:
+        @pl.when(is_remote)
+        def _():
+            pl.semaphore_signal(barrier, 1, device_id=(s, i, r), device_id_type=MESH)
+    for cs, is_remote in sources:
+        @pl.when(is_remote)
+        def _():
+            pl.semaphore_signal(barrier, 1, device_id=(s, c, cs), device_id_type=MESH)
+    for flag, dev in ((has_up, up_id), (has_down, down_id)):
+        @pl.when(flag)
+        def _():
+            pl.semaphore_signal(barrier, 1, device_id=dev, device_id_type=MESH)
+    peers = [p for _, p, _ in dests] + [p for _, p in sources] + [has_up, has_down]
     pl.semaphore_wait(barrier, sum(p.astype(jnp.int32) for p in peers))
 
-    spans = {0: (0, th, TOP), 1: (th - TOP, TOP, 0), -1: (0, BOTTOM, TOP + th)}
     remote_copies = []
-    for i, k, delta, cd, valid, is_self in dests:
-        r0, n, d0 = spans[delta]
-        src = img_ref.at[i, pl.ds(r0, n)]
-        dst = out_ref.at[pl.ds(d0, n), c]
-        slot = 1 - delta
+    for i, is_remote, is_self in dests:
+        src = img_ref.at[i]
+        dst = out_ref.at[pl.ds(TOP, th), c]
         rdesc = pltpu.make_async_remote_copy(
             src_ref=src,
             dst_ref=dst,
-            send_sem=send_sem.at[i, k],
-            recv_sem=recv_sem.at[slot, c],
-            device_id=(s, i, cd),
+            send_sem=send_sem.at[i],
+            recv_sem=recv_sem.at[c],
+            device_id=(s, i, r),
             device_id_type=MESH,
         )
-        ldesc = pltpu.make_async_copy(src, dst, recv_sem.at[slot, c])
-        is_remote = remote(valid, is_self)
+        ldesc = pltpu.make_async_copy(src, dst, recv_sem.at[c])
 
         @pl.when(is_remote)
         def _():
             rdesc.start()
 
-        @pl.when(jnp.logical_and(valid, is_self))
+        @pl.when(is_self)
         def _():
             ldesc.start()
 
         remote_copies.append((rdesc, is_remote))
 
-    lands = {0: (TOP, 0), 1: (th, TOP), 2: (BOTTOM, TOP + th)}
-    for d, cs, rs, valid, is_self in sources:
-        n, d0 = lands[d]
-        dst = out_ref.at[pl.ds(d0, n), cs]
-        desc = pltpu.make_async_copy(dst, dst, recv_sem.at[d, cs])
-
-        @pl.when(valid)
-        def _():
-            desc.wait()
+    for cs, _ in sources:
+        dst = out_ref.at[pl.ds(TOP, th), cs]
+        pltpu.make_async_copy(dst, dst, recv_sem.at[cs]).wait()
+
+    to_up = pltpu.make_async_remote_copy(
+        src_ref=out_ref.at[pl.ds(TOP, BOTTOM)],
+        dst_ref=out_ref.at[pl.ds(TOP + th, BOTTOM)],
+        send_sem=fwd_send.at[0],
+        recv_sem=fwd_recv.at[1],
+        device_id=up_id,
+        device_id_type=MESH,
+    )
+    to_down = pltpu.make_async_remote_copy(
+        src_ref=out_ref.at[pl.ds(TOP + th - TOP, TOP)],
+        dst_ref=out_ref.at[pl.ds(0, TOP)],
+        send_sem=fwd_send.at[1],
+        recv_sem=fwd_recv.at[0],
+        device_id=down_id,
+        device_id_type=MESH,
+    )
+
+    @pl.when(has_up)
+    def _():
+        to_up.start()
+
+    @pl.when(has_down)
+    def _():
+        to_down.start()
+
+    @pl.when(has_down)
+    def _():
+        pltpu.make_async_copy(to_up.dst_ref, to_up.dst_ref, fwd_recv.at[1]).wait()
+
+    @pl.when(has_up)
+    def _():
+        pltpu.make_async_copy(to_down.dst_ref, to_down.dst_ref, fwd_recv.at[0]).wait()
 
     for rdesc, is_remote in remote_copies:
         @pl.when(is_remote)
         def _():
             rdesc.wait_send()
+
+    @pl.when(has_up)
+    def _():
+        to_up.wait_send()
+
+    @pl.when(has_down)
+    def _():
+        to_down.wait_send()
 
 
 def gather_strips(tiles, nrow, ncol):
@@ -111,16 +142,13 @@
         in_specs=[pl.BlockSpec(memory_space=pl.ANY)],
         out_specs=pl.BlockSpec(memory_space=pl.ANY),
         scratch_shapes=[
-            pltpu.SemaphoreType.DMA((n_img, 3)),
-            pltpu.SemaphoreType.DMA((3, ncol)),
+            pltpu.SemaphoreType.DMA((n_img,)),
+            pltpu.SemaphoreType.DMA((ncol,)),
+            pltpu.SemaphoreType.DMA((2,)),
+            pltpu.SemaphoreType.DMA((2,)),
         ],
         compiler_params=pltpu.CompilerParams(collective_id=0, has_side_effects=True),
     )(tiles)
-
-
-def tap_weights(weight):
-    channels = weight.shape[1]
-    return weight.reshape(3, 3, GROUP, channels).transpose(1, 0, 2, 3).reshape(3, 3 * GROUP, channels)
 
 
 def inside_rows(count, width, first, height):
@@ -136,7 +164,11 @@
     sl = slice(group * GROUP, (group + 1) * GROUP)
     slab = jnp.concatenate([rows_of(a)[:, :, sl] for a in range(3)], axis=-1)
     slab = slab.reshape(out_rows * width, 3 * GROUP).astype(jnp.bfloat16)
-    return [jnp.dot(slab, w_ref[b, :, sl], preferred_element_type=jnp.float32) for b in range(3)]
+    outs = []
+    for b in range(3):
+        taps = jnp.concatenate([w_ref[(3 * a + b) * GROUP : (3 * a + b + 1) * GROUP, sl] for a in range(3)], axis=0)
+        outs.append(jnp.dot(slab, taps, preferred_element_type=jnp.float32))
+    return outs
 
 
 def conv_same(x, w_ref):
@@ -229,7 +261,7 @@
             trans_in, trans_grouped_one, trans_grouped_two, trans_out, trans_short):
     rows, width, ch = strip.shape
     block_result = vmem_call(block_kernel, jax.ShapeDtypeStruct((rows - 4, width, ch), jnp.bfloat16), 5)(
-        base_info, strip, block_in, tap_weights(block_grouped_one), tap_weights(block_grouped_two), block_out
+        base_info, strip, block_in, block_grouped_one, block_grouped_two, block_out
     )
     t_rows = rows - 4
     core_rows = t_rows - 5
@@ -242,7 +274,7 @@
     )
     out_shape = jax.ShapeDtypeStruct(((core_rows // 2) * (width // 2), wide), jnp.bfloat16)
     features = vmem_call(trans_kernel, out_shape, 6, scratch)(
-        base_info, block_result, trans_in, tap_weights(trans_grouped_one), tap_weights(trans_grouped_two),
+        base_info, block_result, trans_in, trans_grouped_one, trans_grouped_two,
         trans_out, trans_short
     )
     return features.reshape(core_rows // 2, width // 2, wide)

time: 117 us -> 97.3 us (0.83)
  the two profiles are of different devices: /device:TPU:92 before, /device:TPU:240 now
where the time goes in v1:
time: 97.3 us; the launch traced here: 97.1 us
  Pallas kernels  89.6 us (92%)
  local copies, waits for them, and re-layouts  6.87 us (7%)
    pallas_call x1, Pallas kernels, gather_strips(): pl.pallas_call(functools.partial(gather_kernel, nrow, ncol), out_shape=ja...  67.9 us
    pallas_call x1, Pallas kernels, compute(): vmem_call(trans_kernel, out_shape, 6, scratch)  11.8 us
    pallas_call x1, Pallas kernels, compute(): vmem_call(block_kernel, jax.ShapeDtypeStruct((rows - 4, width, ch), jnp.b...  9.84 us
    pallas_call x1, local copies, waits for them, and re-layouts, gather_strips(): pl.pallas_call(functools.partial(gather_kernel, nrow, ncol), out_shape=ja...  2.66 us
    unnamed x1, local copies, waits for them, and re-layouts  2.54 us

profile of v1, /device:TPU:240, one launch (start us, length us, event | category | flops | bytes accessed | tf_op | source)
XLA Modules:
  0.0 97.1 jit_solution(6345831939074917832)
XLA Ops:
  0.0 0.6 pad_add_fusion.base_ref
  0.6 2.5 %copy.16 = bf16[1,8,10,10,512]{4,3,2,1,0:T(8,128)(2,1)} copy(bf16[1,8,10,10,512]{4,1,3,2,0:T(8,128)(2,1)} %param.10) | data formatting | bytes 1638400 | tf_op args[0]
  3.2 67.9 %shard_map.100 = bf16[19,8,10,512]{3,2,1,0:T(8,128)(2,1)} custom-call(bf16[8,10,10,512]{3,2,1,0:T(8,128)(2,1)} %bitcast.7), custom_call_target="tpu_custom_call" | custom-call | tf_op jit(solution)/shard_map/pallas_call | solution.py:139
  71.1 2.7 %copy.13 = bf16[19,8,10,512]{3,0,2,1:T(8,128)(2,1)S(1)} copy(bf16[19,8,10,512]{3,2,1,0:T(8,128)(2,1)} %shard_map.100) | data formatting | bytes 3112960 | tf_op jit(solution)/shard_map/pallas_call | solution.py:139
  73.8 1.7 %copy.14.x_ref = bf16[19,80,512]{2,1,0:T(8,128)(2,1)} copy(bf16[19,80,512]{2,0,1:T(8,128)(2,1)S(1)} %bitcast.6) | data formatting | bytes 3112960 | tf_op jit(solution)/shard_map/reshape | solution.py:301
  75.5 9.8 %shard_map.101.x_ref = bf16[15,80,512]{2,1,0:T(8,128)(2,1)} custom-call(s32[2]{0:T(128)} %pad_add_fusion.base_ref, bf16[19,80,512]{2,1,0:T(8,128)(2,1)} %copy.14.x_ref, bf16[512,256]{1,0:T(8,128)(2,1)} %win_ref.2, bf16[1152,256]{1,0:T(8,128)(2,1)} %w1_ref.2, bf16[1152,256]{1,0:T(8,128)(2,1)} %w2_ref.2, bf16[256,512]{1,0:T(8,128)(2,1)} %wout_ref.2), custom_call_target="tpu_custom_call" | custom-call | tf_op jit(solution)/shard_map/pallas_call | solution.py:263
  85.3 11.8 %shard_map.102 = bf16[200,1536]{1,0:T(8,128)(2,1)} custom-call(s32[2]{0:T(128)} %pad_add_fusion.base_ref, bf16[15,80,512]{2,1,0:T(8,128)(2,1)} %shard_map.101.x_ref, bf16[512,768]{1,0:T(8,128)(2,1)} %win_ref.3, bf16[1152,768]{1,0:T(8,128)(2,1)} %w1_ref.3, bf16[1152,768]{1,0:T(8,128)(2,1)} %w2_ref.3, bf16[768,1536]{1,0:T(8,128)(2,1)} %wout_ref.3, ...), custom_call_target="tpu_custom_call" | custom-call | tf_op jit(solution)/shard_map/pallas_call | solution.py:276

commit v2 on v1

--- a/solution.py
+++ b/solution.py
@@ -60,78 +60,86 @@
     pl.semaphore_wait(barrier, sum(p.astype(jnp.int32) for p in peers))
 
     remote_copies = []
-    for i, is_remote, is_self in dests:
+    for k in range(n_img):
+        i = lax.rem(c + k, n_img)
         src = img_ref.at[i]
         dst = out_ref.at[pl.ds(TOP, th), c]
         rdesc = pltpu.make_async_remote_copy(
             src_ref=src,
             dst_ref=dst,
-            send_sem=send_sem.at[i],
+            send_sem=send_sem.at[k],
             recv_sem=recv_sem.at[c],
             device_id=(s, i, r),
             device_id_type=MESH,
         )
-        ldesc = pltpu.make_async_copy(src, dst, recv_sem.at[c])
+        is_self = jnp.logical_and(r == c, k == 0)
+        is_remote = jnp.logical_not(is_self)
 
         @pl.when(is_remote)
         def _():
             rdesc.start()
 
-        @pl.when(is_self)
-        def _():
-            ldesc.start()
+        if k == 0:
+            @pl.when(is_self)
+            def _():
+                pltpu.make_async_copy(src, dst, recv_sem.at[c]).start()
 
         remote_copies.append((rdesc, is_remote))
 
-    for cs, _ in sources:
+    forwards = []
+    for k in range(ncol):
+        cs = lax.rem(r - k + ncol, ncol)
         dst = out_ref.at[pl.ds(TOP, th), cs]
         pltpu.make_async_copy(dst, dst, recv_sem.at[cs]).wait()
-
-    to_up = pltpu.make_async_remote_copy(
-        src_ref=out_ref.at[pl.ds(TOP, BOTTOM)],
-        dst_ref=out_ref.at[pl.ds(TOP + th, BOTTOM)],
-        send_sem=fwd_send.at[0],
-        recv_sem=fwd_recv.at[1],
-        device_id=up_id,
-        device_id_type=MESH,
-    )
-    to_down = pltpu.make_async_remote_copy(
-        src_ref=out_ref.at[pl.ds(TOP + th - TOP, TOP)],
-        dst_ref=out_ref.at[pl.ds(0, TOP)],
-        send_sem=fwd_send.at[1],
-        recv_sem=fwd_recv.at[0],
-        device_id=down_id,
-        device_id_type=MESH,
-    )
-
-    @pl.when(has_up)
-    def _():
-        to_up.start()
-
-    @pl.when(has_down)
-    def _():
-        to_down.start()
-
-    @pl.when(has_down)
-    def _():
-        pltpu.make_async_copy(to_up.dst_ref, to_up.dst_ref, fwd_recv.at[1]).wait()
-
-    @pl.when(has_up)
-    def _():
-        pltpu.make_async_copy(to_down.dst_ref, to_down.dst_ref, fwd_recv.at[0]).wait()
+        to_up = pltpu.make_async_remote_copy(
+            src_ref=out_ref.at[pl.ds(TOP, BOTTOM), cs],
+            dst_ref=out_ref.at[pl.ds(TOP + th, BOTTOM), cs],
+            send_sem=fwd_send.at[0, k],
+            recv_sem=fwd_recv.at[1, cs],
+            device_id=up_id,
+            device_id_type=MESH,
+        )
+        to_down = pltpu.make_async_remote_copy(
+            src_ref=out_ref.at[pl.ds(th, TOP), cs],
+            dst_ref=out_ref.at[pl.ds(0, TOP), cs],
+            send_sem=fwd_send.at[1, k],
+            recv_sem=fwd_recv.at[0, cs],
+            device_id=down_id,
+            device_id_type=MESH,
+        )
+
+        @pl.when(has_up)
+        def _():
+            to_up.start()
+
+        @pl.when(has_down)
+        def _():
+            to_down.start()
+
+        forwards.append((to_up, to_down, cs))
+
+    for to_up, to_down, cs in forwards:
+        @pl.when(has_down)
+        def _():
+            pltpu.make_async_copy(to_up.dst_ref, to_up.dst_ref, fwd_recv.at[1, cs]).wait()
+
+        @pl.when(has_up)
+        def _():
+            pltpu.make_async_copy(to_down.dst_ref, to_down.dst_ref, fwd_recv.at[0, cs]).wait()
 
     for rdesc, is_remote in remote_copies:
         @pl.when(is_remote)
         def _():
             rdesc.wait_send()
 
-    @pl.when(has_up)
-    def _():
-        to_up.wait_send()
-
-    @pl.when(has_down)
-    def _():
-        to_down.wait_send()
+    for to_up, to_down, cs in forwards:
+        @pl.when(has_up)
+        def _():
+            to_up.wait_send()
+
+        @pl.when(has_down)
+        def _():
+            to_down.wait_send()
 
 
 def gather_strips(tiles, nrow, ncol):
@@ -144,8 +152,8 @@
         scratch_shapes=[
             pltpu.SemaphoreType.DMA((n_img,)),
             pltpu.SemaphoreType.DMA((ncol,)),
-            pltpu.SemaphoreType.DMA((2,)),
-            pltpu.SemaphoreType.DMA((2,)),
+            pltpu.SemaphoreType.DMA((2, ncol)),
+            pltpu.SemaphoreType.DMA((2, ncol)),
         ],
         compiler_params=pltpu.CompilerParams(collective_id=0, has_side_effects=True),
     )(tiles)

time: 97.3 us -> 86.2 us (0.89)
  the two profiles are of different devices: /device:TPU:240 before, /device:TPU:59 now
where the time goes in v2:
time: 86.2 us; the launch traced here: 86 us
  Pallas kernels  78.5 us (91%)
  local copies, waits for them, and re-layouts  6.87 us (8%)
    pallas_call x1, Pallas kernels, gather_strips(): pl.pallas_call(functools.partial(gather_kernel, nrow, ncol), out_shape=ja...  56.8 us
    pallas_call x1, Pallas kernels, compute(): vmem_call(trans_kernel, out_shape, 6, scratch)  11.8 us
    pallas_call x1, Pallas kernels, compute(): vmem_call(block_kernel, jax.ShapeDtypeStruct((rows - 4, width, ch), jnp.b...  9.84 us
    pallas_call x1, local copies, waits for them, and re-layouts, gather_strips(): pl.pallas_call(functools.partial(gather_kernel, nrow, ncol), out_shape=ja...  2.66 us
    unnamed x1, local copies, waits for them, and re-layouts  2.54 us

profile of v2, /device:TPU:59, one launch (start us, length us, event | category | flops | bytes accessed | tf_op | source)
XLA Modules:
  0.0 86.0 jit_solution(7312287384935194281)
XLA Ops:
  0.0 0.6 pad_add_fusion.base_ref
  0.6 2.5 %copy.16 = bf16[1,8,10,10,512]{4,3,2,1,0:T(8,128)(2,1)} copy(bf16[1,8,10,10,512]{4,1,3,2,0:T(8,128)(2,1)} %param.10) | data formatting | bytes 1638400 | tf_op args[0]
  3.2 56.8 %shard_map.100 = bf16[19,8,10,512]{3,2,1,0:T(8,128)(2,1)} custom-call(bf16[8,10,10,512]{3,2,1,0:T(8,128)(2,1)} %bitcast.7), custom_call_target="tpu_custom_call" | custom-call | tf_op jit(solution)/shard_map/pallas_call | solution.py:147
  60.0 2.7 %copy.13 = bf16[19,8,10,512]{3,0,2,1:T(8,128)(2,1)S(1)} copy(bf16[19,8,10,512]{3,2,1,0:T(8,128)(2,1)} %shard_map.100) | data formatting | bytes 3112960 | tf_op jit(solution)/shard_map/pallas_call | solution.py:147
  62.7 1.7 %copy.14.x_ref = bf16[19,80,512]{2,1,0:T(8,128)(2,1)} copy(bf16[19,80,512]{2,0,1:T(8,128)(2,1)S(1)} %bitcast.6) | data formatting | bytes 3112960 | tf_op jit(solution)/shard_map/reshape | solution.py:309
  64.3 9.8 %shard_map.101.x_ref = bf16[15,80,512]{2,1,0:T(8,128)(2,1)} custom-call(s32[2]{0:T(128)} %pad_add_fusion.base_ref, bf16[19,80,512]{2,1,0:T(8,128)(2,1)} %copy.14.x_ref, bf16[512,256]{1,0:T(8,128)(2,1)} %win_ref.2, bf16[1152,256]{1,0:T(8,128)(2,1)} %w1_ref.2, bf16[1152,256]{1,0:T(8,128)(2,1)} %w2_ref.2, bf16[256,512]{1,0:T(8,128)(2,1)} %wout_ref.2), custom_call_target="tpu_custom_call" | custom-call | tf_op jit(solution)/shard_map/pallas_call | solution.py:271
  74.2 11.8 %shard_map.102 = bf16[200,1536]{1,0:T(8,128)(2,1)} custom-call(s32[2]{0:T(128)} %pad_add_fusion.base_ref, bf16[15,80,512]{2,1,0:T(8,128)(2,1)} %shard_map.101.x_ref, bf16[512,768]{1,0:T(8,128)(2,1)} %win_ref.3, bf16[1152,768]{1,0:T(8,128)(2,1)} %w1_ref.3, bf16[1152,768]{1,0:T(8,128)(2,1)} %w2_ref.3, bf16[768,1536]{1,0:T(8,128)(2,1)} %wout_ref.3, ...), custom_call_target="tpu_custom_call" | custom-call | tf_op jit(solution)/shard_map/pallas_call | solution.py:284

commit v3 on v2

--- a/solution.py
+++ b/solution.py
@@ -193,12 +193,9 @@
     return jnp.concatenate(outs, axis=-1)
 
 
-def block_kernel(base_ref, x_ref, win_ref, w1_ref, w2_ref, wout_ref, o_ref):
-    rows, width, ch = x_ref.shape
-    height = base_ref[1]
-    base = base_ref[0]
-    x = x_ref[...].astype(jnp.float32).reshape(rows * width, ch)
-    pre = (activate(x) * BETA_BLOCK).astype(jnp.bfloat16)
+def block_body(base, height, x, win_ref, w1_ref, w2_ref, wout_ref):
+    rows, width, ch = x.shape
+    pre = (activate(x.reshape(rows * width, ch)) * BETA_BLOCK).astype(jnp.bfloat16)
     first = activate(jnp.dot(pre, win_ref[...], preferred_element_type=jnp.float32))
     first = jnp.where(inside_rows(rows, width, base, height), first, 0.0)
     first = first.astype(jnp.bfloat16).astype(jnp.float32).reshape(rows, width, -1)
@@ -206,18 +203,23 @@
     second = jnp.where(inside_rows(rows - 2, width, base + 1, height), second, 0.0)
     second = second.astype(jnp.bfloat16).astype(jnp.float32).reshape(rows - 2, width, -1)
     third = activate(conv_same(second, w2_ref)).astype(jnp.bfloat16)
-    skip = x_ref[2 : rows - 2].astype(jnp.float32).reshape((rows - 4) * width, ch)
+    skip = x[2 : rows - 2].reshape((rows - 4) * width, ch)
     out = skip + RESIDUAL_SCALE * jnp.dot(third, wout_ref[...], preferred_element_type=jnp.float32)
-    o_ref[...] = out.astype(o_ref.dtype).reshape(rows - 4, width, ch)
-
-
-def trans_kernel(base_ref, x_ref, win_ref, w1_ref, w2_ref, wout_ref, wshort_ref, o_ref, pool_scr, sub_scr):
-    rows, width, ch = x_ref.shape
+    return out.astype(jnp.bfloat16)
+
+
+def fused_kernel(base_ref, x_ref, bin_ref, b1_ref, b2_ref, bout_ref,
+                 win_ref, w1_ref, w2_ref, wout_ref, wshort_ref, o_ref, pool_scr, sub_scr):
+    in_rows, blocks, block_width, ch = x_ref.shape
+    strip = jnp.concatenate([x_ref[:, cb].astype(jnp.float32) for cb in range(blocks)], axis=1)
+    height = base_ref[1]
+    block_result = block_body(base_ref[0], height, strip, bin_ref, b1_ref, b2_ref, bout_ref)
+    rows = in_rows - 4
+    width = blocks * block_width
     core_rows = rows - 5
     half = width // 2
-    height = base_ref[1]
     base = base_ref[0] + 2
-    x = x_ref[...].astype(jnp.float32).reshape(rows * width, ch)
+    x = block_result.astype(jnp.float32)
     pre = (activate(x) * BETA_TRANSITION).astype(jnp.bfloat16)
 
     core = pre.astype(jnp.float32).reshape(rows, width, ch)[2 : 2 + core_rows]
@@ -267,11 +269,9 @@
 
 def compute(strip, base_info, block_in, block_grouped_one, block_grouped_two, block_out,
             trans_in, trans_grouped_one, trans_grouped_two, trans_out, trans_short):
-    rows, width, ch = strip.shape
-    block_result = vmem_call(block_kernel, jax.ShapeDtypeStruct((rows - 4, width, ch), jnp.bfloat16), 5)(
-        base_info, strip, block_in, block_grouped_one, block_grouped_two, block_out
-    )
-    t_rows = rows - 4
+    in_rows, blocks, block_width, ch = strip.shape
+    width = blocks * block_width
+    t_rows = in_rows - 4
     core_rows = t_rows - 5
     out_rows = (t_rows - 1) // 2
     mid = trans_in.shape[1]
@@ -281,9 +281,9 @@
         pltpu.VMEM((mid // GROUP, out_rows * width + 8, GROUP), jnp.float32),
     )
     out_shape = jax.ShapeDtypeStruct(((core_rows // 2) * (width // 2), wide), jnp.bfloat16)
-    features = vmem_call(trans_kernel, out_shape, 6, scratch)(
-        base_info, block_result, trans_in, trans_grouped_one, trans_grouped_two,
-        trans_out, trans_short
+    features = vmem_call(fused_kernel, out_shape, 10, scratch)(
+        base_info, strip, block_in, block_grouped_one, block_grouped_two, block_out,
+        trans_in, trans_grouped_one, trans_grouped_two, trans_out, trans_short
     )
     return features.reshape(core_rows // 2, width // 2, wide)
 
@@ -306,7 +306,6 @@
     c = lax.axis_index("col")
     base_info = jnp.stack([c * th - TOP, th * nrow]).astype(jnp.int32)
     strip = gather_strips(images.reshape(n_img, th, tw, ch), nrow, ncol)
-    strip = strip.reshape(TOP + th + BOTTOM, ncol * tw, ch)
     features = compute(strip, base_info, block_in, block_grouped_one, block_grouped_two, block_out,
                        trans_in, trans_grouped_one, trans_grouped_two, trans_out, trans_short)
     return features[None, None]

time: 86.2 us -> 79.8 us (0.926)
  local copies, waits for them, and re-layouts: 6.87 us -> 2.54 us
  Pallas kernels: 78.5 us -> 76.5 us
    pallas_call x1 -> x0, local copies, waits for them, and re-layouts: 2.66 us -> none  [gather_strips(): pl.pallas_call(functools.partial(gather_kernel, nrow, ncol), out_shape=ja...]
    pallas_call x2 -> x1, Pallas kernels: 21.7 us -> 19.7 us  [compute(): vmem_call(fused_kernel, out_shape, 10, scratch)]
    reshape x1 -> x0, local copies, waits for them, and re-layouts: 1.68 us -> none  [local(): strip = strip.reshape(TOP + th + BOTTOM, ncol * tw, ch)]
where the time goes in v3:
time: 79.8 us; the launch traced here: 79.7 us
  Pallas kernels  76.5 us (96%)
  local copies, waits for them, and re-layouts  2.54 us (3%)
    pallas_call x1, Pallas kernels, gather_strips(): pl.pallas_call(functools.partial(gather_kernel, nrow, ncol), out_shape=ja...  56.8 us
    pallas_call x1, Pallas kernels, compute(): vmem_call(fused_kernel, out_shape, 10, scratch)  19.7 us
    unnamed x1, local copies, waits for them, and re-layouts  2.54 us

profile of v3, /device:TPU:59, one launch (start us, length us, event | category | flops | bytes accessed | tf_op | source)
XLA Modules:
  0.0 79.7 jit_solution(12199435173871901148)
XLA Ops:
  0.0 2.5 %copy.13 = bf16[1,8,10,10,512]{4,3,2,1,0:T(8,128)(2,1)} copy(bf16[1,8,10,10,512]{4,1,3,2,0:T(8,128)(2,1)} %param.10) | data formatting | bytes 1638400 | tf_op args[0]
  2.5 56.8 %shard_map.100.x_ref = bf16[19,8,10,512]{3,2,1,0:T(8,128)(2,1)} custom-call(bf16[8,10,10,512]{3,2,1,0:T(8,128)(2,1)} %bitcast.5), custom_call_target="tpu_custom_call" | custom-call | tf_op jit(solution)/shard_map/pallas_call | solution.py:147
  59.4 0.6 pad_add_fusion.base_ref
  60.0 19.7 %shard_map.101 = bf16[200,1536]{1,0:T(8,128)(2,1)} custom-call(s32[2]{0:T(128)} %pad_add_fusion.base_ref, bf16[19,8,10,512]{3,2,1,0:T(8,128)(2,1)} %shard_map.100.x_ref, bf16[512,256]{1,0:T(8,128)(2,1)} %bin_ref.1, bf16[1152,256]{1,0:T(8,128)(2,1)} %b1_ref.1, bf16[1152,256]{1,0:T(8,128)(2,1)} %b2_ref.1, bf16[256,512]{1,0:T(8,128)(2,1)} %bout_ref.1, ...), custom_call_target="tpu_custom_call" | custom-call | tf_op jit(solution)/shard_map/pallas_call | solution.py:284

commit v4 on v3

--- a/solution.py
+++ b/solution.py
@@ -210,12 +210,11 @@
 
 def fused_kernel(base_ref, x_ref, bin_ref, b1_ref, b2_ref, bout_ref,
                  win_ref, w1_ref, w2_ref, wout_ref, wshort_ref, o_ref, pool_scr, sub_scr):
-    in_rows, blocks, block_width, ch = x_ref.shape
-    strip = jnp.concatenate([x_ref[:, cb].astype(jnp.float32) for cb in range(blocks)], axis=1)
+    in_rows, width, ch = x_ref.shape
+    strip = x_ref[...].astype(jnp.float32)
     height = base_ref[1]
     block_result = block_body(base_ref[0], height, strip, bin_ref, b1_ref, b2_ref, bout_ref)
     rows = in_rows - 4
-    width = blocks * block_width
     core_rows = rows - 5
     half = width // 2
     base = base_ref[0] + 2
@@ -269,8 +268,7 @@
 
 def compute(strip, base_info, block_in, block_grouped_one, block_grouped_two, block_out,
             trans_in, trans_grouped_one, trans_grouped_two, trans_out, trans_short):
-    in_rows, blocks, block_width, ch = strip.shape
-    width = blocks * block_width
+    in_rows, width, ch = strip.shape
     t_rows = in_rows - 4
     core_rows = t_rows - 5
     out_rows = (t_rows - 1) // 2
@@ -305,7 +303,8 @@
     _, n_img, th, tw, ch = images.shape
     c = lax.axis_index("col")
     base_info = jnp.stack([c * th - TOP, th * nrow]).astype(jnp.int32)
-    strip = gather_strips(images.reshape(n_img, th, tw, ch), nrow, ncol)
+    tiles = images.reshape(n_img, th, tw * (ch // GROUP), GROUP)
+    strip = gather_strips(tiles, nrow, ncol).reshape(TOP + th + BOTTOM, ncol * tw, ch)
     features = compute(strip, base_info, block_in, block_grouped_one, block_grouped_two, block_out,
                        trans_in, trans_grouped_one, trans_grouped_two, trans_out, trans_short)
     return features[None, None]

time: 79.8 us -> 65.9 us (0.83)
  the two profiles are of different devices: /device:TPU:59 before, /device:TPU:24 now
where the time goes in v4:
time: 65.9 us; the launch traced here: 65.8 us
  Pallas kernels  58.6 us (89%)
  local copies, waits for them, and re-layouts  6.51 us (10%)
  other arithmetic  0.66 us (1%)
    pallas_call x1, Pallas kernels, gather_strips(): pl.pallas_call(functools.partial(gather_kernel, nrow, ncol), out_shape=ja...  39.7 us
    pallas_call x1, Pallas kernels, compute(): vmem_call(fused_kernel, out_shape, 10, scratch)  18.9 us
    reshape x1, local copies, waits for them, and re-layouts, local(): gather_strips(tiles, nrow, ncol).reshape(TOP + th + BOTTOM, ncol * tw, ch)  3.71 us
    unnamed x1, local copies, waits for them, and re-layouts  1.45 us
    reshape x1, local copies, waits for them, and re-layouts, local(): tiles = images.reshape(n_img, th, tw * (ch // GROUP), GROUP)  1.35 us

profile of v4, /device:TPU:24, one launch (start us, length us, event | category | flops | bytes accessed | tf_op | source)
XLA Modules:
  0.0 65.8 jit_solution(4883003724381151489)
XLA Ops:
  0.0 1.5 %copy.12 = bf16[1,8,10,10,512]{4,3,2,1,0:T(8,128)(2,1)S(1)} copy(bf16[1,8,10,10,512]{4,1,3,2,0:T(8,128)(2,1)} %param.10) | data formatting | bytes 1638400 | tf_op args[0]
  1.5 1.3 %reshape.6.img_ref = bf16[8,10,40,128]{3,2,1,0:T(8,128)(2,1)} reshape(bf16[1,8,10,10,512]{4,3,2,1,0:T(8,128)(2,1)S(1)} %copy.12) | data formatting | bytes 1638400 | tf_op jit(solution)/shard_map/reshape | solution.py:306
  2.8 39.7 %shard_map.100 = bf16[19,8,40,128]{3,2,1,0:T(8,128)(2,1)} custom-call(bf16[8,10,40,128]{3,2,1,0:T(8,128)(2,1)} %reshape.6.img_ref), custom_call_target="tpu_custom_call" | custom-call | tf_op jit(solution)/shard_map/pallas_call | solution.py:147
  42.5 3.7 %reshape.7.x_ref = bf16[19,80,512]{2,1,0:T(8,128)(2,1)} reshape(bf16[19,8,40,128]{3,2,1,0:T(8,128)(2,1)} %shard_map.100) | data formatting | bytes 3112960 | tf_op jit(solution)/shard_map/reshape | solution.py:307
  46.2 0.7 %pad_add_fusion.base_ref = s32[2]{0:T(128)} fusion(s32[1]{0:T(128)} %constant.10.clone.1, s32[1]{0:T(128)} %bitcast), kind=kLoop, calls=%fused_computation | loop fusion | flops 2 | bytes 16 | tf_op jit(solution)/shard_map/stack | solution.py:305
  46.9 18.9 %shard_map.101 = bf16[200,1536]{1,0:T(8,128)(2,1)} custom-call(s32[2]{0:T(128)} %pad_add_fusion.base_ref, bf16[19,80,512]{2,1,0:T(8,128)(2,1)} %reshape.7.x_ref, bf16[512,256]{1,0:T(8,128)(2,1)} %bin_ref.1, bf16[1152,256]{1,0:T(8,128)(2,1)} %b1_ref.1, bf16[1152,256]{1,0:T(8,128)(2,1)} %b2_ref.1, bf16[256,512]{1,0:T(8,128)(2,1)} %bout_ref.1, ...), custom_call_target="tpu_custom_call" | custom-call | tf_op jit(solution)/shard_map/pallas_call | solution.py:282

commit v5 on v4

--- a/solution.py
+++ b/solution.py
@@ -22,11 +22,11 @@
     return GELU_GAIN * jax.nn.gelu(values, approximate=True)
 
 
-def gather_kernel(nrow, ncol, img_ref, out_ref, send_sem, recv_sem, fwd_send, fwd_recv):
+def gather_kernel(nrow, ncol, th, unit, img_ref, out_ref, send_sem, recv_sem, fwd_send, fwd_recv):
     s = lax.axis_index("section")
     r = lax.axis_index("row")
     c = lax.axis_index("col")
-    n_img, th, tw = img_ref.shape[0], img_ref.shape[1], img_ref.shape[2]
+    n_img = img_ref.shape[0]
     barrier = pltpu.get_barrier_semaphore()
 
     dests = []
@@ -63,7 +63,7 @@
     for k in range(n_img):
         i = lax.rem(c + k, n_img)
         src = img_ref.at[i]
-        dst = out_ref.at[pl.ds(TOP, th), c]
+        dst = out_ref.at[c, pl.ds(TOP * unit, th * unit)]
         rdesc = pltpu.make_async_remote_copy(
             src_ref=src,
             dst_ref=dst,
@@ -89,19 +89,19 @@
     forwards = []
     for k in range(ncol):
         cs = lax.rem(r - k + ncol, ncol)
-        dst = out_ref.at[pl.ds(TOP, th), cs]
+        dst = out_ref.at[cs, pl.ds(TOP * unit, th * unit)]
         pltpu.make_async_copy(dst, dst, recv_sem.at[cs]).wait()
         to_up = pltpu.make_async_remote_copy(
-            src_ref=out_ref.at[pl.ds(TOP, BOTTOM), cs],
-            dst_ref=out_ref.at[pl.ds(TOP + th, BOTTOM), cs],
+            src_ref=out_ref.at[cs, pl.ds(TOP * unit, BOTTOM * unit)],
+            dst_ref=out_ref.at[cs, pl.ds((TOP + th) * unit, BOTTOM * unit)],
             send_sem=fwd_send.at[0, k],
             recv_sem=fwd_recv.at[1, cs],
             device_id=up_id,
             device_id_type=MESH,
         )
         to_down = pltpu.make_async_remote_copy(
-            src_ref=out_ref.at[pl.ds(th, TOP), cs],
-            dst_ref=out_ref.at[pl.ds(0, TOP), cs],
+            src_ref=out_ref.at[cs, pl.ds(th * unit, TOP * unit)],
+            dst_ref=out_ref.at[cs, pl.ds(0, TOP * unit)],
             send_sem=fwd_send.at[1, k],
             recv_sem=fwd_recv.at[0, cs],
             device_id=down_id,
@@ -142,11 +142,12 @@
             to_down.wait_send()
 
 
-def gather_strips(tiles, nrow, ncol):
-    n_img, th, tw, ch = tiles.shape
+def gather_strips(tiles, nrow, ncol, th):
+    n_img, flat, lanes = tiles.shape
+    unit = flat // th
     return pl.pallas_call(
-        functools.partial(gather_kernel, nrow, ncol),
-        out_shape=jax.ShapeDtypeStruct((TOP + th + BOTTOM, ncol, tw, ch), tiles.dtype),
+        functools.partial(gather_kernel, nrow, ncol, th, unit),
+        out_shape=jax.ShapeDtypeStruct((ncol, (TOP + th + BOTTOM) * unit, lanes), tiles.dtype),
         in_specs=[pl.BlockSpec(memory_space=pl.ANY)],
         out_specs=pl.BlockSpec(memory_space=pl.ANY),
         scratch_shapes=[
@@ -303,8 +304,9 @@
     _, n_img, th, tw, ch = images.shape
     c = lax.axis_index("col")
     base_info = jnp.stack([c * th - TOP, th * nrow]).astype(jnp.int32)
-    tiles = images.reshape(n_img, th, tw * (ch // GROUP), GROUP)
-    strip = gather_strips(tiles, nrow, ncol).reshape(TOP + th + BOTTOM, ncol * tw, ch)
+    tiles = images.reshape(n_img, th * tw * (ch // GROUP), GROUP)
+    strip = gather_strips(tiles, nrow, ncol, th).reshape(ncol, TOP + th + BOTTOM, tw, ch)
+    strip = strip.transpose(1, 0, 2, 3).reshape(TOP + th + BOTTOM, ncol * tw, ch)
     features = compute(strip, base_info, block_in, block_grouped_one, block_grouped_two, block_out,
                        trans_in, trans_grouped_one, trans_grouped_two, trans_out, trans_short)
     return features[None, None]

time: 65.9 us -> 67.7 us (1.027)
  local copies, waits for them, and re-layouts: 6.51 us -> 8.2 us
    transpose x0 -> x1, local copies, waits for them, and re-layouts: none -> 0.95 us  [local(): strip.transpose(1, 0, 2, 3).reshape(TOP + th + BOTTOM, ncol * tw, ch)]
    reshape x2 -> x3, local copies, waits for them, and re-layouts: 5.06 us -> 5.79 us  [the longest x1 2.77 us: local(): gather_strips(tiles, nrow, ncol, th)]
where the time goes in v5:
time: 67.7 us; the launch traced here: 67.6 us
  Pallas kernels  58.8 us (87%)
  local copies, waits for them, and re-layouts  8.2 us (12%)
    pallas_call x1, Pallas kernels, gather_strips(): pl.pallas_call(functools.partial(gather_kernel, nrow, ncol, th, unit), ou...  39.7 us
    pallas_call x1, Pallas kernels, compute(): vmem_call(fused_kernel, out_shape, 10, scratch)  19.1 us
    reshape x1, local copies, waits for them, and re-layouts, local(): gather_strips(tiles, nrow, ncol, th)  2.77 us
    reshape x1, local copies, waits for them, and re-layouts, local(): strip.transpose(1, 0, 2, 3).reshape(TOP + th + BOTTOM, ncol * tw, ch)  1.68 us
    unnamed x1, local copies, waits for them, and re-layouts  1.45 us

profile of v5, /device:TPU:24, one launch (start us, length us, event | category | flops | bytes accessed | tf_op | source)
XLA Modules:
  0.0 67.6 jit_solution(6962142824224526486)
XLA Ops:
  0.0 1.5 %copy.13 = bf16[1,8,10,10,512]{4,3,2,1,0:T(8,128)(2,1)S(1)} copy(bf16[1,8,10,10,512]{4,1,3,2,0:T(8,128)(2,1)} %param.10) | data formatting | bytes 1638400 | tf_op args[0]
  1.5 1.3 %reshape.9.img_ref = bf16[8,400,128]{2,1,0:T(8,128)(2,1)} reshape(bf16[1,8,10,10,512]{4,3,2,1,0:T(8,128)(2,1)S(1)} %copy.13) | data formatting | bytes 1638400 | tf_op jit(solution)/shard_map/reshape | solution.py:307
  2.8 39.7 %shard_map.100 = bf16[8,760,128]{2,1,0:T(8,128)(2,1)} custom-call(bf16[8,400,128]{2,1,0:T(8,128)(2,1)} %reshape.9.img_ref), custom_call_target="tpu_custom_call" | custom-call | tf_op jit(solution)/shard_map/pallas_call | solution.py:148
  42.5 2.8 %reshape.10 = bf16[8,19,10,512]{3,2,1,0:T(8,128)(2,1)S(1)} reshape(bf16[8,760,128]{2,1,0:T(8,128)(2,1)} %shard_map.100) | data formatting | bytes 3112960 | tf_op jit(solution)/shard_map/reshape | solution.py:308
  45.3 1.0 %copy.14 = bf16[19,8,10,512]{3,0,2,1:T(8,128)(2,1)S(1)} copy(bf16[19,8,10,512]{3,2,0,1:T(8,128)(2,1)S(1)} %bitcast.4) | data formatting | bytes 3112960 | tf_op jit(solution)/shard_map/transpose | solution.py:309
  46.2 1.7 %copy.15.x_ref = bf16[19,80,512]{2,1,0:T(8,128)(2,1)} copy(bf16[19,80,512]{2,0,1:T(8,128)(2,1)S(1)} %bitcast.5) | data formatting | bytes 3112960 | tf_op jit(solution)/shard_map/reshape | solution.py:309
  47.9 0.6 pad_add_fusion.base_ref
  48.5 19.1 %shard_map.101 = bf16[200,1536]{1,0:T(8,128)(2,1)} custom-call(s32[2]{0:T(128)} %pad_add_fusion.base_ref, bf16[19,80,512]{2,1,0:T(8,128)(2,1)} %copy.15.x_ref, bf16[512,256]{1,0:T(8,128)(2,1)} %bin_ref.1, bf16[1152,256]{1,0:T(8,128)(2,1)} %b1_ref.1, bf16[1152,256]{1,0:T(8,128)(2,1)} %b2_ref.1, bf16[256,512]{1,0:T(8,128)(2,1)} %bout_ref.1, ...), custom_call_target="tpu_custom_call" | custom-call | tf_op jit(solution)/shard_map/pallas_call | solution.py:283

commit v6 on v4

--- a/solution.py
+++ b/solution.py
@@ -172,11 +172,12 @@
     sl = slice(group * GROUP, (group + 1) * GROUP)
     slab = jnp.concatenate([rows_of(a)[:, :, sl] for a in range(3)], axis=-1)
     slab = slab.reshape(out_rows * width, 3 * GROUP).astype(jnp.bfloat16)
-    outs = []
-    for b in range(3):
-        taps = jnp.concatenate([w_ref[(3 * a + b) * GROUP : (3 * a + b + 1) * GROUP, sl] for a in range(3)], axis=0)
-        outs.append(jnp.dot(slab, taps, preferred_element_type=jnp.float32))
-    return outs
+    taps = [
+        jnp.concatenate([w_ref[(3 * a + b) * GROUP : (3 * a + b + 1) * GROUP, sl] for a in range(3)], axis=0)
+        for b in range(3)
+    ]
+    y = jnp.dot(slab, jnp.concatenate(taps, axis=1), preferred_element_type=jnp.float32)
+    return [y[:, b * GROUP : (b + 1) * GROUP] for b in range(3)]
 
 
 def conv_same(x, w_ref):

time: 65.9 us -> 63.6 us (0.965)
  Pallas kernels: 58.6 us -> 56.3 us
    pallas_call x1, Pallas kernels: 18.9 us -> 16.6 us  [compute(): vmem_call(fused_kernel, out_shape, 10, scratch)]
where the time goes in v6:
time: 63.6 us; the launch traced here: 63.5 us
  Pallas kernels  56.3 us (89%)
  local copies, waits for them, and re-layouts  6.51 us (10%)
  other arithmetic  0.66 us (1%)
    pallas_call x1, Pallas kernels, gather_strips(): pl.pallas_call(functools.partial(gather_kernel, nrow, ncol), out_shape=ja...  39.7 us
    pallas_call x1, Pallas kernels, compute(): vmem_call(fused_kernel, out_shape, 10, scratch)  16.6 us
    reshape x1, local copies, waits for them, and re-layouts, local(): gather_strips(tiles, nrow, ncol).reshape(TOP + th + BOTTOM, ncol * tw, ch)  3.71 us
    unnamed x1, local copies, waits for them, and re-layouts  1.45 us
    reshape x1, local copies, waits for them, and re-layouts, local(): tiles = images.reshape(n_img, th, tw * (ch // GROUP), GROUP)  1.35 us

profile of v6, /device:TPU:24, one launch (start us, length us, event | category | flops | bytes accessed | tf_op | source)
XLA Modules:
  0.0 63.5 jit_solution(9047096919939836120)
XLA Ops:
  0.0 1.5 %copy.12 = bf16[1,8,10,10,512]{4,3,2,1,0:T(8,128)(2,1)S(1)} copy(bf16[1,8,10,10,512]{4,1,3,2,0:T(8,128)(2,1)} %param.10) | data formatting | bytes 1638400 | tf_op args[0]
  1.5 1.3 %reshape.6.img_ref = bf16[8,10,40,128]{3,2,1,0:T(8,128)(2,1)} reshape(bf16[1,8,10,10,512]{4,3,2,1,0:T(8,128)(2,1)S(1)} %copy.12) | data formatting | bytes 1638400 | tf_op jit(solution)/shard_map/reshape | solution.py:307
  2.8 39.7 %shard_map.100 = bf16[19,8,40,128]{3,2,1,0:T(8,128)(2,1)} custom-call(bf16[8,10,40,128]{3,2,1,0:T(8,128)(2,1)} %reshape.6.img_ref), custom_call_target="tpu_custom_call" | custom-call | tf_op jit(solution)/shard_map/pallas_call | solution.py:147
  42.5 3.7 %reshape.7.x_ref = bf16[19,80,512]{2,1,0:T(8,128)(2,1)} reshape(bf16[19,8,40,128]{3,2,1,0:T(8,128)(2,1)} %shard_map.100) | data formatting | bytes 3112960 | tf_op jit(solution)/shard_map/reshape | solution.py:308
  46.2 0.7 %pad_add_fusion.base_ref = s32[2]{0:T(128)} fusion(s32[1]{0:T(128)} %constant.10.clone.1, s32[1]{0:T(128)} %bitcast), kind=kLoop, calls=%fused_computation | loop fusion | flops 2 | bytes 16 | tf_op jit(solution)/shard_map/stack | solution.py:306
  46.9 16.6 %shard_map.101 = bf16[200,1536]{1,0:T(8,128)(2,1)} custom-call(s32[2]{0:T(128)} %pad_add_fusion.base_ref, bf16[19,80,512]{2,1,0:T(8,128)(2,1)} %reshape.7.x_ref, bf16[512,256]{1,0:T(8,128)(2,1)} %bin_ref.1, bf16[1152,256]{1,0:T(8,128)(2,1)} %b1_ref.1, bf16[1152,256]{1,0:T(8,128)(2,1)} %b2_ref.1, bf16[256,512]{1,0:T(8,128)(2,1)} %bout_ref.1, ...), custom_call_target="tpu_custom_call" | custom-call | tf_op jit(solution)/shard_map/pallas_call | solution.py:283

commit v7 on v6

--- a/solution.py
+++ b/solution.py
@@ -1,4 +1,5 @@
 import functools
+import math
 
 import jax
 import jax.numpy as jnp
@@ -13,13 +14,16 @@
 BETA_TRANSITION = 0.9623
 GROUP = 128
 MESH = pl.DeviceIdType.MESH
+TANH_SCALE = math.sqrt(2.0 / math.pi)
 
 TOP = 4
 BOTTOM = 5
 
 
-def activate(values):
-    return GELU_GAIN * jax.nn.gelu(values, approximate=True)
+def activate(values, scale=1.0):
+    inner = values * (TANH_SCALE + TANH_SCALE * 0.044715 * (values * values))
+    half = values * (0.5 * GELU_GAIN * scale)
+    return half + half * jnp.tanh(inner)
 
 
 def gather_kernel(nrow, ncol, img_ref, out_ref, send_sem, recv_sem, fwd_send, fwd_recv):
@@ -196,7 +200,7 @@
 
 def block_body(base, height, x, win_ref, w1_ref, w2_ref, wout_ref):
     rows, width, ch = x.shape
-    pre = (activate(x.reshape(rows * width, ch)) * BETA_BLOCK).astype(jnp.bfloat16)
+    pre = activate(x.reshape(rows * width, ch), BETA_BLOCK).astype(jnp.bfloat16)
     first = activate(jnp.dot(pre, win_ref[...], preferred_element_type=jnp.float32))
     first = jnp.where(inside_rows(rows, width, base, height), first, 0.0)
     first = first.astype(jnp.bfloat16).astype(jnp.float32).reshape(rows, width, -1)
@@ -220,7 +224,7 @@
     half = width // 2
     base = base_ref[0] + 2
     x = block_result.astype(jnp.float32)
-    pre = (activate(x) * BETA_TRANSITION).astype(jnp.bfloat16)
+    pre = activate(x, BETA_TRANSITION).astype(jnp.bfloat16)
 
     core = pre.astype(jnp.float32).reshape(rows, width, ch)[2 : 2 + core_rows]
     core = core.reshape(core_rows // 2, 2, width, ch)

time: 63.6 us -> 62.8 us (0.987)
  Pallas kernels: 56.3 us -> 55.5 us
    pallas_call x1, Pallas kernels: 16.6 us -> 15.8 us  [compute(): vmem_call(fused_kernel, out_shape, 10, scratch)]
where the time goes in v7:
time: 62.8 us; the launch traced here: 62.7 us
  Pallas kernels  55.5 us (88%)
  local copies, waits for them, and re-layouts  6.51 us (10%)
  other arithmetic  0.66 us (1%)
    pallas_call x1, Pallas kernels, gather_strips(): pl.pallas_call(functools.partial(gather_kernel, nrow, ncol), out_shape=ja...  39.7 us
    pallas_call x1, Pallas kernels, compute(): vmem_call(fused_kernel, out_shape, 10, scratch)  15.8 us
    reshape x1, local copies, waits for them, and re-layouts, local(): gather_strips(tiles, nrow, ncol).reshape(TOP + th + BOTTOM, ncol * tw, ch)  3.71 us
    unnamed x1, local copies, waits for them, and re-layouts  1.45 us
    reshape x1, local copies, waits for them, and re-layouts, local(): tiles = images.reshape(n_img, th, tw * (ch // GROUP), GROUP)  1.35 us

profile of v7, /device:TPU:24, one launch (start us, length us, event | category | flops | bytes accessed | tf_op | source)
XLA Modules:
  0.0 62.7 jit_solution(15396474277593667186)
XLA Ops:
  0.0 1.5 %copy.12 = bf16[1,8,10,10,512]{4,3,2,1,0:T(8,128)(2,1)S(1)} copy(bf16[1,8,10,10,512]{4,1,3,2,0:T(8,128)(2,1)} %param.10) | data formatting | bytes 1638400 | tf_op args[0]
  1.5 1.3 %reshape.6.img_ref = bf16[8,10,40,128]{3,2,1,0:T(8,128)(2,1)} reshape(bf16[1,8,10,10,512]{4,3,2,1,0:T(8,128)(2,1)S(1)} %copy.12) | data formatting | bytes 1638400 | tf_op jit(solution)/shard_map/reshape | solution.py:311
  2.8 39.7 %shard_map.100 = bf16[19,8,40,128]{3,2,1,0:T(8,128)(2,1)} custom-call(bf16[8,10,40,128]{3,2,1,0:T(8,128)(2,1)} %reshape.6.img_ref), custom_call_target="tpu_custom_call" | custom-call | tf_op jit(solution)/shard_map/pallas_call | solution.py:151
  42.5 3.7 %reshape.7.x_ref = bf16[19,80,512]{2,1,0:T(8,128)(2,1)} reshape(bf16[19,8,40,128]{3,2,1,0:T(8,128)(2,1)} %shard_map.100) | data formatting | bytes 3112960 | tf_op jit(solution)/shard_map/reshape | solution.py:312
  46.2 0.7 %pad_add_fusion.base_ref = s32[2]{0:T(128)} fusion(s32[1]{0:T(128)} %constant.10.clone.1, s32[1]{0:T(128)} %bitcast), kind=kLoop, calls=%fused_computation | loop fusion | flops 2 | bytes 16 | tf_op jit(solution)/shard_map/stack | solution.py:310
  46.9 15.8 %shard_map.101 = bf16[200,1536]{1,0:T(8,128)(2,1)} custom-call(s32[2]{0:T(128)} %pad_add_fusion.base_ref, bf16[19,80,512]{2,1,0:T(8,128)(2,1)} %reshape.7.x_ref, bf16[512,256]{1,0:T(8,128)(2,1)} %bin_ref.1, bf16[1152,256]{1,0:T(8,128)(2,1)} %b1_ref.1, bf16[1152,256]{1,0:T(8,128)(2,1)} %b2_ref.1, bf16[256,512]{1,0:T(8,128)(2,1)} %bout_ref.1, ...), custom_call_target="tpu_custom_call" | custom-call | tf_op jit(solution)/shard_map/pallas_call | solution.py:287

commit v8 on v7

--- a/solution.py
+++ b/solution.py
@@ -215,8 +215,12 @@
 
 def fused_kernel(base_ref, x_ref, bin_ref, b1_ref, b2_ref, bout_ref,
                  win_ref, w1_ref, w2_ref, wout_ref, wshort_ref, o_ref, pool_scr, sub_scr):
-    in_rows, width, ch = x_ref.shape
-    strip = x_ref[...].astype(jnp.float32)
+    in_rows, blocks, packed, lanes = x_ref.shape
+    ch = bin_ref.shape[0]
+    block_width = packed * lanes // ch
+    width = blocks * block_width
+    pieces = [x_ref[:, cb].astype(jnp.float32).reshape(in_rows, block_width, ch // lanes, lanes) for cb in range(blocks)]
+    strip = jnp.concatenate([p.reshape(in_rows, block_width, ch) for p in pieces], axis=1)
     height = base_ref[1]
     block_result = block_body(base_ref[0], height, strip, bin_ref, b1_ref, b2_ref, bout_ref)
     rows = in_rows - 4
@@ -273,7 +277,9 @@
 
 def compute(strip, base_info, block_in, block_grouped_one, block_grouped_two, block_out,
             trans_in, trans_grouped_one, trans_grouped_two, trans_out, trans_short):
-    in_rows, width, ch = strip.shape
+    in_rows, blocks, packed, lanes = strip.shape
+    ch = block_in.shape[0]
+    width = blocks * packed * lanes // ch
     t_rows = in_rows - 4
     core_rows = t_rows - 5
     out_rows = (t_rows - 1) // 2
@@ -309,7 +315,7 @@
     c = lax.axis_index("col")
     base_info = jnp.stack([c * th - TOP, th * nrow]).astype(jnp.int32)
     tiles = images.reshape(n_img, th, tw * (ch // GROUP), GROUP)
-    strip = gather_strips(tiles, nrow, ncol).reshape(TOP + th + BOTTOM, ncol * tw, ch)
+    strip = gather_strips(tiles, nrow, ncol)
     features = compute(strip, base_info, block_in, block_grouped_one, block_grouped_two, block_out,
                        trans_in, trans_grouped_one, trans_grouped_two, trans_out, trans_short)
     return features[None, None]

time: 62.8 us -> 59.5 us (0.947)
  local copies, waits for them, and re-layouts: 6.51 us -> 2.8 us
    reshape x1 -> x0, local copies, waits for them, and re-layouts: 3.71 us -> none  [local(): gather_strips(tiles, nrow, ncol).reshape(TOP + th + BOTTOM, ncol * tw, ch)]
where the time goes in v8:
time: 59.5 us; the launch traced here: 59.4 us
  Pallas kernels  56 us (94%)
  local copies, waits for them, and re-layouts  2.8 us (5%)
    pallas_call x1, Pallas kernels, gather_strips(): pl.pallas_call(functools.partial(gather_kernel, nrow, ncol), out_shape=ja...  39.7 us
    pallas_call x1, Pallas kernels, compute(): vmem_call(fused_kernel, out_shape, 10, scratch)  16.3 us
    unnamed x1, local copies, waits for them, and re-layouts  1.45 us
    reshape x1, local copies, waits for them, and re-layouts, local(): tiles = images.reshape(n_img, th, tw * (ch // GROUP), GROUP)  1.35 us

profile of v8, /device:TPU:24, one launch (start us, length us, event | category | flops | bytes accessed | tf_op | source)
XLA Modules:
  0.0 59.4 jit_solution(1190195402666375071)
XLA Ops:
  0.0 1.5 %copy.12 = bf16[1,8,10,10,512]{4,3,2,1,0:T(8,128)(2,1)S(1)} copy(bf16[1,8,10,10,512]{4,1,3,2,0:T(8,128)(2,1)} %param.10) | data formatting | bytes 1638400 | tf_op args[0]
  1.5 1.3 %reshape.3.img_ref = bf16[8,10,40,128]{3,2,1,0:T(8,128)(2,1)} reshape(bf16[1,8,10,10,512]{4,3,2,1,0:T(8,128)(2,1)S(1)} %copy.12) | data formatting | bytes 1638400 | tf_op jit(solution)/shard_map/reshape | solution.py:317
  2.8 39.7 %shard_map.100.x_ref = bf16[19,8,40,128]{3,2,1,0:T(8,128)(2,1)} custom-call(bf16[8,10,40,128]{3,2,1,0:T(8,128)(2,1)} %reshape.3.img_ref), custom_call_target="tpu_custom_call" | custom-call | tf_op jit(solution)/shard_map/pallas_call | solution.py:151
  42.5 0.6 pad_add_fusion.base_ref
  43.1 16.3 %shard_map.101 = bf16[200,1536]{1,0:T(8,128)(2,1)} custom-call(s32[2]{0:T(128)} %pad_add_fusion.base_ref, bf16[19,8,40,128]{3,2,1,0:T(8,128)(2,1)} %shard_map.100.x_ref, bf16[512,256]{1,0:T(8,128)(2,1)} %bin_ref.1, bf16[1152,256]{1,0:T(8,128)(2,1)} %b1_ref.1, bf16[1152,256]{1,0:T(8,128)(2,1)} %b2_ref.1, bf16[256,512]{1,0:T(8,128)(2,1)} %bout_ref.1, ...), custom_call_target="tpu_custom_call" | custom-call | tf_op jit(solution)/shard_map/pallas_call | solution.py:293

commit v9 on v8

--- a/solution.py
+++ b/solution.py
@@ -213,7 +213,7 @@
     return out.astype(jnp.bfloat16)
 
 
-def fused_kernel(base_ref, x_ref, bin_ref, b1_ref, b2_ref, bout_ref,
+def fused_kernel(x_ref, bin_ref, b1_ref, b2_ref, bout_ref,
                  win_ref, w1_ref, w2_ref, wout_ref, wshort_ref, o_ref, pool_scr, sub_scr):
     in_rows, blocks, packed, lanes = x_ref.shape
     ch = bin_ref.shape[0]
@@ -221,12 +221,14 @@
     width = blocks * block_width
     pieces = [x_ref[:, cb].astype(jnp.float32).reshape(in_rows, block_width, ch // lanes, lanes) for cb in range(blocks)]
     strip = jnp.concatenate([p.reshape(in_rows, block_width, ch) for p in pieces], axis=1)
-    height = base_ref[1]
-    block_result = block_body(base_ref[0], height, strip, bin_ref, b1_ref, b2_ref, bout_ref)
+    th = in_rows - TOP - BOTTOM
+    height = th * lax.axis_size("row")
+    start = lax.axis_index("col") * th - TOP
+    block_result = block_body(start, height, strip, bin_ref, b1_ref, b2_ref, bout_ref)
     rows = in_rows - 4
     core_rows = rows - 5
     half = width // 2
-    base = base_ref[0] + 2
+    base = start + 2
     x = block_result.astype(jnp.float32)
     pre = activate(x, BETA_TRANSITION).astype(jnp.bfloat16)
 
@@ -257,7 +259,7 @@
         sub_scr[g, pl.ds(0, n), :] = z
     picked = [sub_scr.at[g][pl.ds(0, out_rows * half, stride=2), :] for g in range(mid // GROUP)]
     second = activate(jnp.concatenate(picked, axis=-1))
-    second = jnp.where(inside_rows(out_rows, half, base_ref[0] // 2 + 1, height // 2), second, 0.0)
+    second = jnp.where(inside_rows(out_rows, half, (start + TOP) // 2 - 1, height // 2), second, 0.0)
     second = second.astype(jnp.bfloat16).astype(jnp.float32).reshape(out_rows, half, mid)
     third = activate(conv_same(second, w2_ref)).astype(jnp.bfloat16)
     out = jnp.dot(pooled, wshort_ref[...], preferred_element_type=jnp.float32)
@@ -269,13 +271,13 @@
     return pl.pallas_call(
         kernel,
         out_shape=out_shape,
-        in_specs=[pl.BlockSpec(memory_space=pltpu.SMEM)] + [pl.BlockSpec(memory_space=pltpu.VMEM)] * n_in,
+        in_specs=[pl.BlockSpec(memory_space=pltpu.VMEM)] * n_in,
         out_specs=pl.BlockSpec(memory_space=pltpu.VMEM),
         scratch_shapes=list(scratch),
     )
 
 
-def compute(strip, base_info, block_in, block_grouped_one, block_grouped_two, block_out,
+def compute(strip, block_in, block_grouped_one, block_grouped_two, block_out,
             trans_in, trans_grouped_one, trans_grouped_two, trans_out, trans_short):
     in_rows, blocks, packed, lanes = strip.shape
     ch = block_in.shape[0]
@@ -291,7 +293,7 @@
     )
     out_shape = jax.ShapeDtypeStruct(((core_rows // 2) * (width // 2), wide), jnp.bfloat16)
     features = vmem_call(fused_kernel, out_shape, 10, scratch)(
-        base_info, strip, block_in, block_grouped_one, block_grouped_two, block_out,
+        strip, block_in, block_grouped_one, block_grouped_two, block_out,
         trans_in, trans_grouped_one, trans_grouped_two, trans_out, trans_short
     )
     return features.reshape(core_rows // 2, width // 2, wide)
@@ -312,11 +314,9 @@
     nrow = lax.axis_size("row")
     ncol = lax.axis_size("col")
     _, n_img, th, tw, ch = images.shape
-    c = lax.axis_index("col")
-    base_info = jnp.stack([c * th - TOP, th * nrow]).astype(jnp.int32)
     tiles = images.reshape(n_img, th, tw * (ch // GROUP), GROUP)
     strip = gather_strips(tiles, nrow, ncol)
-    features = compute(strip, base_info, block_in, block_grouped_one, block_grouped_two, block_out,
+    features = compute(strip, block_in, block_grouped_one, block_grouped_two, block_out,
                        trans_in, trans_grouped_one, trans_grouped_two, trans_out, trans_short)
     return features[None, None]
 

time: 59.5 us -> 58.9 us (0.990)
  no operation moved by 1% of the time
where the time goes in v9:
time: 58.9 us; the launch traced here: 58.8 us
  Pallas kernels  56 us (95%)
  local copies, waits for them, and re-layouts  2.8 us (5%)
    pallas_call x1, Pallas kernels, gather_strips(): pl.pallas_call(functools.partial(gather_kernel, nrow, ncol), out_shape=ja...  39.7 us
    pallas_call x1, Pallas kernels, compute(): vmem_call(fused_kernel, out_shape, 10, scratch)  16.3 us
    unnamed x1, local copies, waits for them, and re-layouts  1.45 us
    reshape x1, local copies, waits for them, and re-layouts, local(): tiles = images.reshape(n_img, th, tw * (ch // GROUP), GROUP)  1.35 us

profile of v9, /device:TPU:24, one launch (start us, length us, event | category | flops | bytes accessed | tf_op | source)
XLA Modules:
  0.0 58.8 jit_solution(9812753906262161570)
XLA Ops:
  0.0 1.5 %copy.12 = bf16[1,8,10,10,512]{4,3,2,1,0:T(8,128)(2,1)S(1)} copy(bf16[1,8,10,10,512]{4,1,3,2,0:T(8,128)(2,1)} %param.10) | data formatting | bytes 1638400 | tf_op args[0]
  1.5 1.3 %reshape.3.img_ref = bf16[8,10,40,128]{3,2,1,0:T(8,128)(2,1)} reshape(bf16[1,8,10,10,512]{4,3,2,1,0:T(8,128)(2,1)S(1)} %copy.12) | data formatting | bytes 1638400 | tf_op jit(solution)/shard_map/reshape | solution.py:317
  2.8 39.7 %shard_map.100.x_ref = bf16[19,8,40,128]{3,2,1,0:T(8,128)(2,1)} custom-call(bf16[8,10,40,128]{3,2,1,0:T(8,128)(2,1)} %reshape.3.img_ref), custom_call_target="tpu_custom_call" | custom-call | tf_op jit(solution)/shard_map/pallas_call | solution.py:151
  42.5 16.3 %shard_map.101 = bf16[200,1536]{1,0:T(8,128)(2,1)} custom-call(bf16[19,8,40,128]{3,2,1,0:T(8,128)(2,1)} %shard_map.100.x_ref, bf16[512,256]{1,0:T(8,128)(2,1)} %bin_ref.1, bf16[1152,256]{1,0:T(8,128)(2,1)} %b1_ref.1, bf16[1152,256]{1,0:T(8,128)(2,1)} %b2_ref.1, bf16[256,512]{1,0:T(8,128)(2,1)} %bout_ref.1, bf16[512,768]{1,0:T(8,128)(2,1)} %win_ref.1, ...), custom_call_target="tpu_custom_call" | custom-call | tf_op jit(solution)/shard_map/pallas_call | solution.py:295

commit v10 on v9

--- a/solution.py
+++ b/solution.py
@@ -247,18 +247,34 @@
     first = jnp.where(inside_rows(rows, width, base, height), first, 0.0)
     first = first.astype(jnp.bfloat16).astype(jnp.float32).reshape(rows, width, -1)
     mid = first.shape[-1]
-    first = jnp.concatenate([first, jnp.zeros((1, width, mid), jnp.float32)], axis=0)
-    pairs = first.reshape((rows + 1) // 2, 2, width, mid)
+    first = first.reshape(rows * width, mid)
     out_rows = (rows - 1) // 2
-    picks = (pairs[:out_rows, 0], pairs[:out_rows, 1], pairs[1 : out_rows + 1, 0])
-    n = out_rows * width
-    col = column_of(out_rows, width)
+    n = out_rows * half
+    col = column_of(out_rows, half)
+    outs = []
     for g in range(mid // GROUP):
-        y = conv_taps(lambda a: picks[a], out_rows, width, w1_ref, g)
-        z = y[0] + pltpu.roll(y[1], n - 1, 0) + jnp.where(col >= width - 2, 0.0, pltpu.roll(y[2], n - 2, 0))
-        sub_scr[g, pl.ds(0, n), :] = z
-    picked = [sub_scr.at[g][pl.ds(0, out_rows * half, stride=2), :] for g in range(mid // GROUP)]
-    second = activate(jnp.concatenate(picked, axis=-1))
+        sl = slice(g * GROUP, (g + 1) * GROUP)
+        sub_scr[g, pl.ds(0, rows * width), :] = first[:, sl]
+        sub_scr[g, pl.ds(rows * width, width), :] = jnp.zeros((width, GROUP), jnp.float32)
+        planes = [
+            sub_scr.at[g][pl.ds(p, (rows + 1) * half, stride=2), :].reshape((rows + 1) // 2, 2, half, GROUP)
+            for p in range(2)
+        ]
+        slabs = [
+            jnp.concatenate([q[:out_rows, 0], q[:out_rows, 1], q[1 : out_rows + 1, 0]], axis=-1)
+            .reshape(n, 3 * GROUP)
+            .astype(jnp.bfloat16)
+            for q in planes
+        ]
+        taps = [
+            jnp.concatenate([w1_ref[(3 * a + b) * GROUP : (3 * a + b + 1) * GROUP, sl] for a in range(3)], axis=0)
+            for b in range(3)
+        ]
+        ye = jnp.dot(slabs[0], jnp.concatenate([taps[0], taps[2]], axis=1), preferred_element_type=jnp.float32)
+        yo = jnp.dot(slabs[1], taps[1], preferred_element_type=jnp.float32)
+        right = jnp.where(col == half - 1, 0.0, pltpu.roll(ye[:, GROUP:], n - 1, 0))
+        outs.append(ye[:, :GROUP] + yo + right)
+    second = activate(jnp.concatenate(outs, axis=-1))
     second = jnp.where(inside_rows(out_rows, half, (start + TOP) // 2 - 1, height // 2), second, 0.0)
     second = second.astype(jnp.bfloat16).astype(jnp.float32).reshape(out_rows, half, mid)
     third = activate(conv_same(second, w2_ref)).astype(jnp.bfloat16)
@@ -289,7 +305,7 @@
     wide = trans_out.shape[1]
     scratch = (
         pltpu.VMEM((ch // GROUP, core_rows // 2 * width, GROUP), jnp.float32),
-        pltpu.VMEM((mid // GROUP, out_rows * width + 8, GROUP), jnp.float32),
+        pltpu.VMEM((mid // GROUP, (t_rows + 1) * width, GROUP), jnp.float32),
     )
     out_shape = jax.ShapeDtypeStruct(((core_rows // 2) * (width // 2), wide), jnp.bfloat16)
     features = vmem_call(fused_kernel, out_shape, 10, scratch)(

time: 58.9 us -> 58.5 us (level)
  no operation moved by 1% of the time
where the time goes in v10:
time: 58.5 us; the launch traced here: 58.4 us
  Pallas kernels  55.6 us (95%)
  local copies, waits for them, and re-layouts  2.8 us (5%)
    pallas_call x1, Pallas kernels, gather_strips(): pl.pallas_call(functools.partial(gather_kernel, nrow, ncol), out_shape=ja...  39.7 us
    pallas_call x1, Pallas kernels, compute(): vmem_call(fused_kernel, out_shape, 10, scratch)  15.9 us
    unnamed x1, local copies, waits for them, and re-layouts  1.45 us
    reshape x1, local copies, waits for them, and re-layouts, local(): tiles = images.reshape(n_img, th, tw * (ch // GROUP), GROUP)  1.35 us

profile of v10, /device:TPU:24, one launch (start us, length us, event | category | flops | bytes accessed | tf_op | source)
XLA Modules:
  0.0 58.4 jit_solution(9151689638974308426)
XLA Ops:
  0.0 1.5 %copy.12 = bf16[1,8,10,10,512]{4,3,2,1,0:T(8,128)(2,1)S(1)} copy(bf16[1,8,10,10,512]{4,1,3,2,0:T(8,128)(2,1)} %param.10) | data formatting | bytes 1638400 | tf_op args[0]
  1.5 1.3 %reshape.3.img_ref = bf16[8,10,40,128]{3,2,1,0:T(8,128)(2,1)} reshape(bf16[1,8,10,10,512]{4,3,2,1,0:T(8,128)(2,1)S(1)} %copy.12) | data formatting | bytes 1638400 | tf_op jit(solution)/shard_map/reshape | solution.py:333
  2.8 39.7 %shard_map.100.x_ref = bf16[19,8,40,128]{3,2,1,0:T(8,128)(2,1)} custom-call(bf16[8,10,40,128]{3,2,1,0:T(8,128)(2,1)} %reshape.3.img_ref), custom_call_target="tpu_custom_call" | custom-call | tf_op jit(solution)/shard_map/pallas_call | solution.py:151
  42.5 15.9 %shard_map.101 = bf16[200,1536]{1,0:T(8,128)(2,1)} custom-call(bf16[19,8,40,128]{3,2,1,0:T(8,128)(2,1)} %shard_map.100.x_ref, bf16[512,256]{1,0:T(8,128)(2,1)} %bin_ref.1, bf16[1152,256]{1,0:T(8,128)(2,1)} %b1_ref.1, bf16[1152,256]{1,0:T(8,128)(2,1)} %b2_ref.1, bf16[256,512]{1,0:T(8,128)(2,1)} %bout_ref.1, bf16[512,768]{1,0:T(8,128)(2,1)} %win_ref.1, ...), custom_call_target="tpu_custom_call" | custom-call | tf_op jit(solution)/shard_map/pallas_call | solution.py:311
